TPU v7x, 32 devices: a whole 2x2x4 slice. The times are simulated.
32 devices in a mesh: gx: 4 (over z), gy: 8 (over y, x, core).
Axes of the slice: x: 2, y: 2, z: 4, core: 2. Of those that a mesh axis runs over, the one named last changes fastest.
Arguments:
- conductivity: bfloat16 [2, 1024, 4096], P(None, 'gy', 'gx'), may hold values from 0.099609375 to 1.59375
Outputs:
- coarse_stencil: float32 [9, 8, 64, 2048], P(None, 'gy', 'gx')
All inputs are finite; a program needn't handle non-finite values.
Results may differ from a plain program's by a relative error of at most 0.0003.
Values may be sent and summed in bfloat16 or wider, within the bound.
A program may use at most 64 MiB of HBM per device.

v0:
```python
from functools import partial
import jax
import jax.numpy as jnp
from jax import lax
from jax.sharding import PartitionSpec as P


def with_halo(cells, sides, width):
    for axis, dim in sides:
        count = lax.axis_size(axis)
        ends = count - 1
        head = lax.slice_in_dim(cells, 0, width, axis=dim)
        tail = lax.slice_in_dim(cells, cells.shape[dim] - width, cells.shape[dim], axis=dim)
        cells = jnp.concatenate(
            [
                lax.ppermute(tail, axis, [(i, (i + 1) % count) for i in range(ends)]),
                cells,
                lax.ppermute(head, axis, [((i + 1) % count, i) for i in range(ends)]),
            ],
            axis=dim,
        )
    return cells


def harmonic(first, second):
    return 2.0 * first * second / (first + second)


def prepare_window(extended, row_start, col_start, rows_all, cols_all, used_rows, used_cols):
    conduct = extended.astype(jnp.float32)
    ext_rows = conduct.shape[1]
    ext_cols = conduct.shape[2]
    row_places = jnp.arange(ext_rows, dtype=jnp.int32)
    col_places = jnp.arange(ext_cols, dtype=jnp.int32)
    row_ids = row_start - 2 + row_places
    col_ids = col_start - 2 + col_places
    row_inside = (row_ids >= 0) & (row_ids < rows_all) & (row_places < used_rows)
    col_inside = (col_ids >= 0) & (col_ids < cols_all) & (col_places < used_cols)
    inside = row_inside[:, None] & col_inside[None, :]
    safe_values = jnp.where(inside[None], conduct, 1.0)
    east_face = jnp.where(
        jnp.roll(inside, -1, 1)[None],
        harmonic(safe_values, jnp.roll(safe_values, -1, 2)),
        safe_values,
    )
    west_face = jnp.where(
        jnp.roll(inside, 1, 1)[None],
        harmonic(safe_values, jnp.roll(safe_values, 1, 2)),
        safe_values,
    )
    north_face = jnp.where(
        jnp.roll(inside, -1, 0)[None],
        harmonic(safe_values, jnp.roll(safe_values, -1, 1)),
        safe_values,
    )
    south_face = jnp.where(
        jnp.roll(inside, 1, 0)[None],
        harmonic(safe_values, jnp.roll(safe_values, 1, 1)),
        safe_values,
    )
    vertical = harmonic(safe_values[0], safe_values[1])
    centre = east_face + west_face + north_face + south_face + vertical[None] + safe_values
    col_east = east_face[0] + east_face[1]
    col_west = west_face[0] + west_face[1]
    row_north = north_face[0] + north_face[1]
    row_south = south_face[0] + south_face[1]
    left_weight = col_west / (col_west + col_east)
    right_weight = col_east / (col_west + col_east)
    south_weight = row_south / (row_south + row_north)
    north_weight = row_north / (row_south + row_north)
    odd_rows = (row_ids % 2 == 1)[:, None]
    odd_cols = (col_ids % 2 == 1)[None, :]
    even_point = inside & (row_ids % 2 == 0)[:, None] & (col_ids % 2 == 0)[None, :]
    row_class = (row_ids // 2 % 3)[:, None]
    col_class = (col_ids // 2 % 3)[None, :]
    return (
        inside,
        odd_rows,
        odd_cols,
        even_point,
        row_class,
        col_class,
        east_face,
        west_face,
        north_face,
        south_face,
        vertical,
        centre,
        left_weight,
        right_weight,
        south_weight,
        north_weight,
    )


def probe_rows(prepared, local_rows, colour):
    (
        inside,
        odd_rows,
        odd_cols,
        even_point,
        row_class,
        col_class,
        east_face,
        west_face,
        north_face,
        south_face,
        vertical,
        centre,
        left_weight,
        right_weight,
        south_weight,
        north_weight,
    ) = prepared
    chosen = even_point & (row_class == colour // 3) & (col_class == colour % 3)
    probe_field = chosen.astype(jnp.float32)
    along_x = jnp.where(
        odd_cols,
        left_weight * jnp.roll(probe_field, 1, 1) + right_weight * jnp.roll(probe_field, -1, 1),
        probe_field,
    )
    fine_field = jnp.where(
        odd_rows,
        south_weight * jnp.roll(along_x, 1, 0) + north_weight * jnp.roll(along_x, -1, 0),
        along_x,
    )
    fine_field = jnp.where(inside, fine_field, 0.0)
    applied = (
        centre * fine_field
        - east_face * jnp.roll(fine_field, -1, 1)
        - west_face * jnp.roll(fine_field, 1, 1)
        - north_face * jnp.roll(fine_field, -1, 0)
        - south_face * jnp.roll(fine_field, 1, 0)
        - vertical * fine_field
    )
    folded = jnp.where(inside, applied[0] + applied[1], 0.0)
    rows_done = (
        folded + jnp.roll(south_weight * folded, -1, 0) + jnp.roll(north_weight * folded, 1, 0)
    )
    cols_done = (
        rows_done
        + jnp.roll(left_weight * rows_done, -1, 1)
        + jnp.roll(right_weight * rows_done, 1, 1)
    )
    width = cols_done.shape[1]
    kept = cols_done[2 : 2 + local_rows].reshape(local_rows // 2, 2, width)
    return kept[:, 0]


def by_offset(colours, row_first, col_first):
    count_rows = colours.shape[1]
    count_cols = colours.shape[2]
    coarse_rows = row_first + jnp.arange(count_rows, dtype=jnp.int32)
    coarse_cols = col_first + jnp.arange(count_cols, dtype=jnp.int32)
    fields = []
    for step_row in (-1, 0, 1):
        for step_col in (-1, 0, 1):
            row_group = (coarse_rows + step_row) % 3
            col_group = (coarse_cols + step_col) % 3
            selected = jnp.zeros((count_rows, count_cols), jnp.float32)
            for colour in range(9):
                chosen = (row_group == colour // 3)[:, None] & (col_group == colour % 3)[None, :]
                selected = jnp.where(chosen, colours[colour], selected)
            fields.append(selected)
    return jnp.stack(fields)


def shards(conductivity):
    local_rows = conductivity.shape[1]
    local_cols = conductivity.shape[2]
    row_start = lax.axis_index("gy") * local_rows
    col_start = lax.axis_index("gx") * local_cols
    rows_all = local_rows * lax.axis_size("gy")
    cols_all = local_cols * lax.axis_size("gx")
    extended = with_halo(conductivity, (("gx", 2), ("gy", 1)), 2)
    used_rows = local_rows + 4
    used_cols = local_cols + 4
    row_fill = -used_rows % 8
    col_fill = -used_cols % 128
    aligned = jnp.pad(extended, ((0, 0), (0, row_fill), (0, col_fill)))
    prepared = prepare_window(
        aligned, row_start, col_start, rows_all, cols_all, used_rows, used_cols
    )
    row_picked = lax.map(partial(probe_rows, prepared, local_rows), jnp.arange(9, dtype=jnp.int32))
    width = row_picked.shape[2]
    half_cols = local_cols // 2
    picker = (
        jnp.arange(width, dtype=jnp.int32)[:, None]
        == 2 + 2 * jnp.arange(half_cols, dtype=jnp.int32)[None, :]
    ).astype(jnp.float32)
    flat_rows = row_picked.reshape(9 * (local_rows // 2), width)
    colours = jnp.dot(
        flat_rows, picker, precision=lax.Precision.HIGHEST, preferred_element_type=jnp.float32
    )
    colours = colours.reshape(9, local_rows // 2, half_cols)
    stencil = by_offset(colours, row_start // 2, col_start // 2)
    moved = lax.all_to_all(stencil, "gx", split_axis=1, concat_axis=2, tiled=True)
    return moved[:, None]


def solution(mesh):
    in_specs = (P(None, "gy", "gx"),)
    out_specs = P(None, "gy", "gx", None)
    return jax.shard_map(shards, mesh=mesh, in_specs=in_specs, out_specs=out_specs, check_vma=False)
```

profile of v0, /device:TPU:4, one launch (start us, length us, event | category | flops | bytes accessed | tf_op | source)
XLA Modules:
  0.0 210.9 jit_solution(8876209915577884419)
XLA Ops:
  1.0 3.5 %collective-permute-start = (bf16[2,128,2]{2,1,0:T(8,128)(2,1)S(1)}, bf16[2,128,2]{2,1,0:T(8,128)(2,1)S(1)}, u32[]{:S(2)}, u32[]{:S(2)}) collective-permute-start(bf16[2,128,2]{2,1,0:T(8,128)(2,1)S(1)} %get-tuple-element.442), channel_id=1, source_target_pairs={{0,8},{8,16},{16,24},{1,9},{9,17},{17,25},{2,10},{10,18},{18,26},{... | collective-permute-start | bytes 3080 | tf_op jit(solution)/shard_map/ppermute | solution.py:16
  4.5 1.3 collective-permute-start.1
  7.1 3.5 %collective-permute-done.1 = bf16[2,128,2]{2,1,0:T(8,128)(2,1)S(1)} collective-permute-done((bf16[2,128,2]{2,1,0:T(8,128)(2,1)S(1)}, bf16[2,128,2]{2,1,0:T(8,128)(2,1)S(1)}, u32[]{:S(2)}, u32[]{:S(2)}) %collective-permute-start.1) | collective-permute-done | bytes 1056 | tf_op jit(solution)/shard_map/ppermute | solution.py:18
  11.3 1.9 collective-permute-start.2
  13.2 4.5 %collective-permute-start.3 = (bf16[2,2,1028]{2,1,0:T(2,128)(2,1)S(1)}, bf16[2,2,1028]{2,1,0:T(2,128)(2,1)S(1)}, u32[]{:S(2)}, u32[]{:S(2)}) collective-permute-start(bf16[2,2,1028]{2,1,0:T(2,128)(2,1)S(1)} %get-tuple-element.440), channel_id=1, source_target_pairs={{1,0},{2,1},{3,2},{4,3},{5,4},{6,5},{7,6},{9,8},{10,9},{11,10},{12... | collective-permute-start | bytes 24680 | tf_op jit(solution)/shard_map/ppermute | solution.py:18
  17.8 1.3 collective-permute-done.3
  21.1 4.2 %add_add_fusion = (f32[2,136,1152]{2,1,0:T(8,128)}, f32[2,136,1152]{2,1,0:T(8,128)S(1)}, f32[2,136,1152]{2,1,0:T(8,128)S(1)}, f32[2,136,1152]{2,1,0:T(8,128)S(1)}, f32[2,136,1152]{2,1,0:T(8,128)S(1)}) fusion(f32[136,1152]{1,0:T(8,128)S(1)} %divide_bitcast_fusion, pred[136,1152]{1,0:T(8,128)(4,1)S(1)} %broadcast_and_fusion, ...), kind=kLoop, calls=%fused_computation.66 | loop fusion | flops 13160448 | bytes 13233216 | tf_op jit(solution)/shard_map/add | solution.py:62
  27.6 121.1 %while.14 = (s32[]{:T(128)}, f32[9,64,1152]{2,1,0:T(8,128)}, s32[9]{0:T(128)S(1)}, f32[136,1152]{1,0:T(8,128)S(1)}, f32[136,1152]{1,0:T(8,128)S(1)}, /*index=5*/...) while((s32[]{:T(128)}, f32[9,64,1152]{2,1,0:T(8,128)}, ...), condition=%wide.region_1.2_spmd.clone.clone, body=%wide.region_0.1_spmd.clone.clone.sunk | while | flops 10339566 | bytes 78140304 | solution.py:184
  31.2 1.4 fusion.104
  37.9 1.2 reshape.701
  39.1 1.3 slice_bitcast_fusion.2
  44.6 1.4 fusion.104
  52.5 1.3 slice_bitcast_fusion.2
  58.1 1.4 fusion.104
  66.0 1.3 slice_bitcast_fusion.2
  71.5 1.4 fusion.104
  78.2 1.2 reshape.701
  79.4 1.3 slice_bitcast_fusion.2
  85.0 1.4 fusion.104
  92.9 1.3 slice_bitcast_fusion.2
  98.4 1.4 fusion.104
  105.1 1.2 reshape.701
  106.3 1.3 slice_bitcast_fusion.2
  111.9 1.4 fusion.104
  119.8 1.3 slice_bitcast_fusion.2
  125.4 1.4 fusion.104
  133.2 1.3 slice_bitcast_fusion.2
  138.8 1.4 fusion.104
  146.7 1.3 slice_bitcast_fusion.2
  148.7 4.3 %fusion.23 = f32[576,512]{1,0:T(8,128)S(1)} fusion(f32[576,1152]{1,0:T(8,128)} %bitcast.88, s32[512]{0:T(512)S(1)} %multiply_add_fusion), kind=kOutput, calls=%fused_computation.55 | convolution fusion | flops 4077453312 | bytes 3835904 | tf_op jit(solution)/shard_map/dot_general | solution.py:192
  155.7 52.7 %all_to_all.15 = f32[9,64,512]{2,0,1:T(8,128)S(1)} all-to-all(f32[9,64,512]{2,0,1:T(8,128)S(1)} %copy.7), channel_id=1, replica_groups=mesh['gx'=4,'gy'=8] {'gx'}, dimensions={1} | all-to-all | bytes 2359296 | tf_op jit(solution)/shard_map/all_to_all | solution.py:197
  209.1 1.8 broadcast_in_dim.97
  (425 shorter events, 86.9 us)
Async XLA Ops:
  1.0 6.1 %collective-permute-start = (bf16[2,128,2]{2,1,0:T(8,128)(2,1)S(1)}, bf16[2,128,2]{2,1,0:T(8,128)(2,1)S(1)}, u32[]{:S(2)}, u32[]{:S(2)}) collective-permute-start(bf16[2,128,2]{2,1,0:T(8,128)(2,1)S(1)} %get-tuple-element.442), channel_id=1, source_target_pairs={{0,8},{8,16},{16,24},{1,9},{9,17},{17,25},{2,10},{10,18},{18,26},{... | collective-permute-start | bytes 3080 | tf_op jit(solution)/shard_map/ppermute | solution.py:16
  4.5 6.2 %collective-permute-start.1 = (bf16[2,128,2]{2,1,0:T(8,128)(2,1)S(1)}, bf16[2,128,2]{2,1,0:T(8,128)(2,1)S(1)}, u32[]{:S(2)}, u32[]{:S(2)}) collective-permute-start(bf16[2,128,2]{2,1,0:T(8,128)(2,1)S(1)} %get-tuple-element.441), channel_id=1, source_target_pairs={{8,0},{16,8},{24,16},{9,1},{17,9},{25,17},{10,2},{18,10},{26,18},{... | collective-permute-start | bytes 3080 | tf_op jit(solution)/shard_map/ppermute | solution.py:18
  5.9 4.7 %copy-start.9 = (bf16[2,128,1024]{2,1,0:T(8,128)(2,1)S(1)}, bf16[2,128,1024]{2,1,0:T(8,128)(2,1)}, u32[]{:S(2)}) copy-start(bf16[2,128,1024]{2,1,0:T(8,128)(2,1)} %param.3) | copy-start | bytes 1572868
  11.3 6.5 %collective-permute-start.2 = (bf16[2,2,1028]{2,1,0:T(2,128)(2,1)S(1)}, bf16[2,2,1028]{2,1,0:T(2,128)(2,1)S(1)}, u32[]{:S(2)}, u32[]{:S(2)}) collective-permute-start(bf16[2,2,1028]{2,1,0:T(2,128)(2,1)S(1)} %get-tuple-element.439), channel_id=1, source_target_pairs={{0,1},{1,2},{2,3},{3,4},{4,5},{5,6},{6,7},{8,9},{9,10},{10,11},{11... | collective-permute-start | bytes 24680 | tf_op jit(solution)/shard_map/ppermute | solution.py:16
  13.2 5.9 %collective-permute-start.3 = (bf16[2,2,1028]{2,1,0:T(2,128)(2,1)S(1)}, bf16[2,2,1028]{2,1,0:T(2,128)(2,1)S(1)}, u32[]{:S(2)}, u32[]{:S(2)}) collective-permute-start(bf16[2,2,1028]{2,1,0:T(2,128)(2,1)S(1)} %get-tuple-element.440), channel_id=1, source_target_pairs={{1,0},{2,1},{3,2},{4,3},{5,4},{6,5},{7,6},{9,8},{10,9},{11,10},{12... | collective-permute-start | bytes 24680 | tf_op jit(solution)/shard_map/ppermute | solution.py:18
  25.3 2.0 copy-start.4
  25.3 2.3 %copy-start.6 = (f32[2,136,1152]{2,1,0:T(8,128)}, f32[2,136,1152]{2,1,0:T(8,128)S(1)}, u32[]{:S(2)}) copy-start(f32[2,136,1152]{2,1,0:T(8,128)S(1)} %get-tuple-element.647) | copy-start | bytes 3760132
  33.3 1.9 copy-start.7
  33.4 2.2 %copy-start.1 = (f32[2,136,1152]{2,1,0:T(8,128)S(1)}, f32[2,136,1152]{2,1,0:T(8,128)}, u32[]{:S(2)}) copy-start(f32[2,136,1152]{2,1,0:T(8,128)} %get-tuple-element.698) | copy-start | bytes 3760132 | tf_op jit(solution)/shard_map/while
  33.4 2.5 %copy-start.3 = (f32[2,136,1152]{2,1,0:T(8,128)S(1)}, f32[2,136,1152]{2,1,0:T(8,128)}, u32[]{:S(2)}) copy-start(f32[2,136,1152]{2,1,0:T(8,128)} %get-tuple-element.699) | copy-start | bytes 3760132 | tf_op jit(solution)/shard_map/while
  46.7 1.9 copy-start.7
  46.8 2.2 %copy-start.1 = (f32[2,136,1152]{2,1,0:T(8,128)S(1)}, f32[2,136,1152]{2,1,0:T(8,128)}, u32[]{:S(2)}) copy-start(f32[2,136,1152]{2,1,0:T(8,128)} %get-tuple-element.698) | copy-start | bytes 3760132 | tf_op jit(solution)/shard_map/while
  46.9 2.5 %copy-start.3 = (f32[2,136,1152]{2,1,0:T(8,128)S(1)}, f32[2,136,1152]{2,1,0:T(8,128)}, u32[]{:S(2)}) copy-start(f32[2,136,1152]{2,1,0:T(8,128)} %get-tuple-element.699) | copy-start | bytes 3760132 | tf_op jit(solution)/shard_map/while
  60.2 1.9 copy-start.7
  60.3 2.2 %copy-start.1 = (f32[2,136,1152]{2,1,0:T(8,128)S(1)}, f32[2,136,1152]{2,1,0:T(8,128)}, u32[]{:S(2)}) copy-start(f32[2,136,1152]{2,1,0:T(8,128)} %get-tuple-element.698) | copy-start | bytes 3760132 | tf_op jit(solution)/shard_map/while
  60.3 2.5 %copy-start.3 = (f32[2,136,1152]{2,1,0:T(8,128)S(1)}, f32[2,136,1152]{2,1,0:T(8,128)}, u32[]{:S(2)}) copy-start(f32[2,136,1152]{2,1,0:T(8,128)} %get-tuple-element.699) | copy-start | bytes 3760132 | tf_op jit(solution)/shard_map/while
  73.6 1.9 copy-start.7
  73.7 2.2 %copy-start.1 = (f32[2,136,1152]{2,1,0:T(8,128)S(1)}, f32[2,136,1152]{2,1,0:T(8,128)}, u32[]{:S(2)}) copy-start(f32[2,136,1152]{2,1,0:T(8,128)} %get-tuple-element.698) | copy-start | bytes 3760132 | tf_op jit(solution)/shard_map/while
  73.8 2.5 %copy-start.3 = (f32[2,136,1152]{2,1,0:T(8,128)S(1)}, f32[2,136,1152]{2,1,0:T(8,128)}, u32[]{:S(2)}) copy-start(f32[2,136,1152]{2,1,0:T(8,128)} %get-tuple-element.699) | copy-start | bytes 3760132 | tf_op jit(solution)/shard_map/while
  87.1 1.9 copy-start.7
  87.2 2.2 %copy-start.1 = (f32[2,136,1152]{2,1,0:T(8,128)S(1)}, f32[2,136,1152]{2,1,0:T(8,128)}, u32[]{:S(2)}) copy-start(f32[2,136,1152]{2,1,0:T(8,128)} %get-tuple-element.698) | copy-start | bytes 3760132 | tf_op jit(solution)/shard_map/while
  87.2 2.5 %copy-start.3 = (f32[2,136,1152]{2,1,0:T(8,128)S(1)}, f32[2,136,1152]{2,1,0:T(8,128)}, u32[]{:S(2)}) copy-start(f32[2,136,1152]{2,1,0:T(8,128)} %get-tuple-element.699) | copy-start | bytes 3760132 | tf_op jit(solution)/shard_map/while
  100.5 1.9 copy-start.7
  100.6 2.2 %copy-start.1 = (f32[2,136,1152]{2,1,0:T(8,128)S(1)}, f32[2,136,1152]{2,1,0:T(8,128)}, u32[]{:S(2)}) copy-start(f32[2,136,1152]{2,1,0:T(8,128)} %get-tuple-element.698) | copy-start | bytes 3760132 | tf_op jit(solution)/shard_map/while
  100.7 2.5 %copy-start.3 = (f32[2,136,1152]{2,1,0:T(8,128)S(1)}, f32[2,136,1152]{2,1,0:T(8,128)}, u32[]{:S(2)}) copy-start(f32[2,136,1152]{2,1,0:T(8,128)} %get-tuple-element.699) | copy-start | bytes 3760132 | tf_op jit(solution)/shard_map/while
  114.1 2.2 %copy-start.1 = (f32[2,136,1152]{2,1,0:T(8,128)S(1)}, f32[2,136,1152]{2,1,0:T(8,128)}, u32[]{:S(2)}) copy-start(f32[2,136,1152]{2,1,0:T(8,128)} %get-tuple-element.698) | copy-start | bytes 3760132 | tf_op jit(solution)/shard_map/while
  114.1 2.5 %copy-start.3 = (f32[2,136,1152]{2,1,0:T(8,128)S(1)}, f32[2,136,1152]{2,1,0:T(8,128)}, u32[]{:S(2)}) copy-start(f32[2,136,1152]{2,1,0:T(8,128)} %get-tuple-element.699) | copy-start | bytes 3760132 | tf_op jit(solution)/shard_map/while
  127.6 2.2 %copy-start.1 = (f32[2,136,1152]{2,1,0:T(8,128)S(1)}, f32[2,136,1152]{2,1,0:T(8,128)}, u32[]{:S(2)}) copy-start(f32[2,136,1152]{2,1,0:T(8,128)} %get-tuple-element.698) | copy-start | bytes 3760132 | tf_op jit(solution)/shard_map/while
  127.6 2.5 %copy-start.3 = (f32[2,136,1152]{2,1,0:T(8,128)S(1)}, f32[2,136,1152]{2,1,0:T(8,128)}, u32[]{:S(2)}) copy-start(f32[2,136,1152]{2,1,0:T(8,128)} %get-tuple-element.699) | copy-start | bytes 3760132 | tf_op jit(solution)/shard_map/while
  140.9 1.9 copy-start.7
  141.0 2.2 %copy-start.1 = (f32[2,136,1152]{2,1,0:T(8,128)S(1)}, f32[2,136,1152]{2,1,0:T(8,128)}, u32[]{:S(2)}) copy-start(f32[2,136,1152]{2,1,0:T(8,128)} %get-tuple-element.698) | copy-start | bytes 3760132 | tf_op jit(solution)/shard_map/while
  141.0 2.5 %copy-start.3 = (f32[2,136,1152]{2,1,0:T(8,128)S(1)}, f32[2,136,1152]{2,1,0:T(8,128)}, u32[]{:S(2)}) copy-start(f32[2,136,1152]{2,1,0:T(8,128)} %get-tuple-element.699) | copy-start | bytes 3760132 | tf_op jit(solution)/shard_map/while
  (22 other events, 31.5 us)
where the time goes:
time: 212 us; the launch traced here: 211 us
  local copies, waits for them, and re-layouts  74.1 us (35%)
  blocking collectives  52.7 us (25%)
  other arithmetic  46.5 us (22%)
  loops' own time  16.9 us (8%)
  starting transfers between devices  11.2 us (5%)
  waiting for transfers between devices  4.81 us (2%)
  matrix products  4.33 us (2%)
    all_to_all x1, blocking collectives, shards(): lax.all_to_all(stencil, 'gx', split_axis=1, concat_axis=2, tiled=True)  52.7 us
    while x90, local copies, waits for them, and re-layouts  21.7 us
    another operation x1, loops' own time, shards(): lax.map(partial(probe_rows, prepared, local_rows), jnp.arange(9, dtype=jn...  16.9 us
    mul x9, other arithmetic, probe_rows(): vertical * fine_field  12.9 us
    broadcast_in_dim x9, local copies, waits for them, and re-layouts, shards(): lax.map(partial(probe_rows, prepared, local_rows), jnp.arange(9, dtype=jn...  11.4 us
    reshape x9, local copies, waits for them, and re-layouts, probe_rows(): kept = cols_done[2:2 + local_rows].reshape(local_rows // 2, 2, width)  10.5 us
    sub x9, other arithmetic, probe_rows(): centre * fine_field - east_face * jnp.roll(fine_field, -1, 1)  6.98 us
    dynamic_update_slice x9, local copies, waits for them, and re-layouts, shards(): lax.map(partial(probe_rows, prepared, local_rows), jnp.arange(9, dtype=jn...  6.72 us
  transfers between devices with their start and end apart: 4, of which 2 were waited for; matrix products, arithmetic and copies ran while one was open for 1% of the time, Pallas kernels for 0%

commit v1 on v0

--- a/solution.py
+++ b/solution.py
@@ -3,6 +3,12 @@
 import jax.numpy as jnp
 from jax import lax
 from jax.sharding import PartitionSpec as P
+
+
+def exchange_blocks(x, mesh_axis, split, join):
+    pieces = jnp.split(x, lax.axis_size(mesh_axis), axis=split)
+    received = lax.all_to_all(jnp.stack(pieces), mesh_axis, 0, 0)
+    return jnp.concatenate(received, axis=join)
 
 
 def with_halo(cells, sides, width):
@@ -194,7 +200,7 @@
     )
     colours = colours.reshape(9, local_rows // 2, half_cols)
     stencil = by_offset(colours, row_start // 2, col_start // 2)
-    moved = lax.all_to_all(stencil, "gx", split_axis=1, concat_axis=2, tiled=True)
+    moved = exchange_blocks(stencil, "gx", 1, 2)
     return moved[:, None]
 
 

time: 212 us -> 196 us (0.925)
  blocking collectives: 52.7 us -> 33 us
  loops' own time: 16.9 us -> 20.1 us
    all_to_all x1, blocking collectives: 52.7 us -> 33 us  [exchange_blocks(): received = lax.all_to_all(jnp.stack(pieces), mesh_axis, 0, 0)]
    another operation x1, loops' own time: 16.9 us -> 20.1 us  [shards(): lax.map(partial(probe_rows, prepared, local_rows), jnp.arange(9, dtype=jn...]
where the time goes in v1:
time: 196 us; the launch traced here: 195 us
  local copies, waits for them, and re-layouts  74.2 us (38%)
  other arithmetic  46.7 us (24%)
  blocking collectives  33 us (17%)
  loops' own time  20.1 us (10%)
  starting transfers between devices  11.2 us (6%)
  waiting for transfers between devices  4.81 us (2%)
  matrix products  4.33 us (2%)
    all_to_all x1, blocking collectives, exchange_blocks(): received = lax.all_to_all(jnp.stack(pieces), mesh_axis, 0, 0)  33 us
    while x90, local copies, waits for them, and re-layouts  21.7 us
    another operation x1, loops' own time, shards(): lax.map(partial(probe_rows, prepared, local_rows), jnp.arange(9, dtype=jn...  20.1 us
    mul x9, other arithmetic, probe_rows(): vertical * fine_field  12.9 us
    broadcast_in_dim x9, local copies, waits for them, and re-layouts, shards(): lax.map(partial(probe_rows, prepared, local_rows), jnp.arange(9, dtype=jn...  11.4 us
    reshape x9, local copies, waits for them, and re-layouts, probe_rows(): kept = cols_done[2:2 + local_rows].reshape(local_rows // 2, 2, width)  10.5 us
    sub x9, other arithmetic, probe_rows(): centre * fine_field - east_face * jnp.roll(fine_field, -1, 1)  6.98 us
    dynamic_update_slice x9, local copies, waits for them, and re-layouts, shards(): lax.map(partial(probe_rows, prepared, local_rows), jnp.arange(9, dtype=jn...  6.71 us
  transfers between devices with their start and end apart: 4, of which 2 were waited for; matrix products, arithmetic and copies ran while one was open for 1% of the time, Pallas kernels for 0%

profile of v1, /device:TPU:4, one launch (start us, length us, event | category | flops | bytes accessed | tf_op | source)
XLA Modules:
  0.0 194.7 jit_solution(8240087640669405069)
XLA Ops:
  1.0 3.5 %collective-permute-start = (bf16[2,128,2]{2,1,0:T(8,128)(2,1)S(1)}, bf16[2,128,2]{2,1,0:T(8,128)(2,1)S(1)}, u32[]{:S(2)}, u32[]{:S(2)}) collective-permute-start(bf16[2,128,2]{2,1,0:T(8,128)(2,1)S(1)} %get-tuple-element.446), channel_id=1, source_target_pairs={{0,8},{8,16},{16,24},{1,9},{9,17},{17,25},{2,10},{10,18},{18,26},{... | collective-permute-start | bytes 3080 | tf_op jit(solution)/shard_map/ppermute | solution.py:22
  4.5 1.3 collective-permute-start.1
  7.1 3.5 %collective-permute-done.1 = bf16[2,128,2]{2,1,0:T(8,128)(2,1)S(1)} collective-permute-done((bf16[2,128,2]{2,1,0:T(8,128)(2,1)S(1)}, bf16[2,128,2]{2,1,0:T(8,128)(2,1)S(1)}, u32[]{:S(2)}, u32[]{:S(2)}) %collective-permute-start.1) | collective-permute-done | bytes 1056 | tf_op jit(solution)/shard_map/ppermute | solution.py:24
  11.3 1.9 collective-permute-start.2
  13.2 4.5 %collective-permute-start.3 = (bf16[2,2,1028]{2,1,0:T(2,128)(2,1)S(1)}, bf16[2,2,1028]{2,1,0:T(2,128)(2,1)S(1)}, u32[]{:S(2)}, u32[]{:S(2)}) collective-permute-start(bf16[2,2,1028]{2,1,0:T(2,128)(2,1)S(1)} %get-tuple-element.444), channel_id=1, source_target_pairs={{1,0},{2,1},{3,2},{4,3},{5,4},{6,5},{7,6},{9,8},{10,9},{11,10},{12... | collective-permute-start | bytes 24680 | tf_op jit(solution)/shard_map/ppermute | solution.py:24
  17.8 1.3 collective-permute-done.3
  21.1 4.2 %add_add_fusion = (f32[2,136,1152]{2,1,0:T(8,128)}, f32[2,136,1152]{2,1,0:T(8,128)S(1)}, f32[2,136,1152]{2,1,0:T(8,128)S(1)}, f32[2,136,1152]{2,1,0:T(8,128)S(1)}, f32[2,136,1152]{2,1,0:T(8,128)S(1)}) fusion(f32[136,1152]{1,0:T(8,128)S(1)} %divide_bitcast_fusion, pred[136,1152]{1,0:T(8,128)(4,1)S(1)} %broadcast_and_fusion, ...), kind=kLoop, calls=%fused_computation.66 | loop fusion | flops 13160448 | bytes 13233216 | tf_op jit(solution)/shard_map/add | solution.py:68
  27.6 125.0 %while.14 = (s32[]{:T(128)}, f32[9,64,1152]{2,1,0:T(8,128)}, s32[9]{0:T(128)S(1)}, f32[136,1152]{1,0:T(8,128)S(1)}, f32[136,1152]{1,0:T(8,128)S(1)}, /*index=5*/...) while((s32[]{:T(128)}, f32[9,64,1152]{2,1,0:T(8,128)}, ...), condition=%wide.region_1.2_spmd.clone.clone, body=%wide.region_0.1_spmd.clone.clone.sunk | while | flops 10339566 | bytes 78140304 | solution.py:190
  31.6 1.4 fusion.104
  38.3 1.2 reshape.704
  39.5 1.3 slice_bitcast_fusion.6
  45.5 1.4 fusion.104
  52.2 1.2 reshape.704
  53.4 1.3 slice_bitcast_fusion.6
  59.4 1.4 fusion.104
  66.1 1.2 reshape.704
  67.3 1.3 slice_bitcast_fusion.6
  73.3 1.4 fusion.104
  81.2 1.3 slice_bitcast_fusion.6
  87.2 1.4 fusion.104
  95.1 1.3 slice_bitcast_fusion.6
  101.0 1.4 fusion.104
  108.9 1.3 slice_bitcast_fusion.6
  115.0 1.4 fusion.104
  122.9 1.3 slice_bitcast_fusion.6
  128.8 1.4 fusion.104
  136.7 1.3 slice_bitcast_fusion.6
  142.7 1.4 fusion.104
  150.6 1.3 slice_bitcast_fusion.6
  152.6 4.3 %fusion.23 = f32[576,512]{1,0:T(8,128)S(1)} fusion(f32[576,1152]{1,0:T(8,128)} %bitcast.95, s32[512]{0:T(512)S(1)} %multiply_add_fusion), kind=kOutput, calls=%fused_computation.55 | convolution fusion | flops 4077453312 | bytes 3835904 | tf_op jit(solution)/shard_map/dot_general | solution.py:198
  159.1 33.0 %all_to_all.5 = f32[4,9,16,512]{3,2,1,0:T(8,128)S(1)} all-to-all(f32[4,9,16,512]{3,2,1,0:T(8,128)S(1)} %pad_maximum_fusion.10), channel_id=1, replica_groups=mesh['gx'=4,'gy'=8] {'gx'}, dimensions={0} | all-to-all | bytes 2359296 | tf_op jit(solution)/shard_map/all_to_all | solution.py:10
  192.9 1.8 broadcast_in_dim_reshape.3
  (426 shorter events, 87.1 us)
Async XLA Ops:
  1.0 6.1 %collective-permute-start = (bf16[2,128,2]{2,1,0:T(8,128)(2,1)S(1)}, bf16[2,128,2]{2,1,0:T(8,128)(2,1)S(1)}, u32[]{:S(2)}, u32[]{:S(2)}) collective-permute-start(bf16[2,128,2]{2,1,0:T(8,128)(2,1)S(1)} %get-tuple-element.446), channel_id=1, source_target_pairs={{0,8},{8,16},{16,24},{1,9},{9,17},{17,25},{2,10},{10,18},{18,26},{... | collective-permute-start | bytes 3080 | tf_op jit(solution)/shard_map/ppermute | solution.py:22
  4.5 6.2 %collective-permute-start.1 = (bf16[2,128,2]{2,1,0:T(8,128)(2,1)S(1)}, bf16[2,128,2]{2,1,0:T(8,128)(2,1)S(1)}, u32[]{:S(2)}, u32[]{:S(2)}) collective-permute-start(bf16[2,128,2]{2,1,0:T(8,128)(2,1)S(1)} %get-tuple-element.445), channel_id=1, source_target_pairs={{8,0},{16,8},{24,16},{9,1},{17,9},{25,17},{10,2},{18,10},{26,18},{... | collective-permute-start | bytes 3080 | tf_op jit(solution)/shard_map/ppermute | solution.py:24
  5.9 4.7 %copy-start.9 = (bf16[2,128,1024]{2,1,0:T(8,128)(2,1)S(1)}, bf16[2,128,1024]{2,1,0:T(8,128)(2,1)}, u32[]{:S(2)}) copy-start(bf16[2,128,1024]{2,1,0:T(8,128)(2,1)} %param.3) | copy-start | bytes 1572868
  11.3 6.5 %collective-permute-start.2 = (bf16[2,2,1028]{2,1,0:T(2,128)(2,1)S(1)}, bf16[2,2,1028]{2,1,0:T(2,128)(2,1)S(1)}, u32[]{:S(2)}, u32[]{:S(2)}) collective-permute-start(bf16[2,2,1028]{2,1,0:T(2,128)(2,1)S(1)} %get-tuple-element.443), channel_id=1, source_target_pairs={{0,1},{1,2},{2,3},{3,4},{4,5},{5,6},{6,7},{8,9},{9,10},{10,11},{11... | collective-permute-start | bytes 24680 | tf_op jit(solution)/shard_map/ppermute | solution.py:22
  13.2 5.9 %collective-permute-start.3 = (bf16[2,2,1028]{2,1,0:T(2,128)(2,1)S(1)}, bf16[2,2,1028]{2,1,0:T(2,128)(2,1)S(1)}, u32[]{:S(2)}, u32[]{:S(2)}) collective-permute-start(bf16[2,2,1028]{2,1,0:T(2,128)(2,1)S(1)} %get-tuple-element.444), channel_id=1, source_target_pairs={{1,0},{2,1},{3,2},{4,3},{5,4},{6,5},{7,6},{9,8},{10,9},{11,10},{12... | collective-permute-start | bytes 24680 | tf_op jit(solution)/shard_map/ppermute | solution.py:24
  25.3 2.0 %copy-start.4 = (f32[2,136,1152]{2,1,0:T(8,128)}, f32[2,136,1152]{2,1,0:T(8,128)S(1)}, u32[]{:S(2)}) copy-start(f32[2,136,1152]{2,1,0:T(8,128)S(1)} %get-tuple-element.650) | copy-start | bytes 3760132
  25.3 2.3 %copy-start.6 = (f32[2,136,1152]{2,1,0:T(8,128)}, f32[2,136,1152]{2,1,0:T(8,128)S(1)}, u32[]{:S(2)}) copy-start(f32[2,136,1152]{2,1,0:T(8,128)S(1)} %get-tuple-element.651) | copy-start | bytes 3760132
  33.7 1.9 copy-start.7
  33.8 2.2 %copy-start.1 = (f32[2,136,1152]{2,1,0:T(8,128)S(1)}, f32[2,136,1152]{2,1,0:T(8,128)}, u32[]{:S(2)}) copy-start(f32[2,136,1152]{2,1,0:T(8,128)} %get-tuple-element.702) | copy-start | bytes 3760132 | tf_op jit(solution)/shard_map/while
  33.8 2.5 %copy-start.3 = (f32[2,136,1152]{2,1,0:T(8,128)S(1)}, f32[2,136,1152]{2,1,0:T(8,128)}, u32[]{:S(2)}) copy-start(f32[2,136,1152]{2,1,0:T(8,128)} %get-tuple-element.703) | copy-start | bytes 3760132 | tf_op jit(solution)/shard_map/while
  47.6 1.9 copy-start.7
  47.7 2.2 %copy-start.1 = (f32[2,136,1152]{2,1,0:T(8,128)S(1)}, f32[2,136,1152]{2,1,0:T(8,128)}, u32[]{:S(2)}) copy-start(f32[2,136,1152]{2,1,0:T(8,128)} %get-tuple-element.702) | copy-start | bytes 3760132 | tf_op jit(solution)/shard_map/while
  47.7 2.5 %copy-start.3 = (f32[2,136,1152]{2,1,0:T(8,128)S(1)}, f32[2,136,1152]{2,1,0:T(8,128)}, u32[]{:S(2)}) copy-start(f32[2,136,1152]{2,1,0:T(8,128)} %get-tuple-element.703) | copy-start | bytes 3760132 | tf_op jit(solution)/shard_map/while
  61.5 1.9 copy-start.7
  61.6 2.2 %copy-start.1 = (f32[2,136,1152]{2,1,0:T(8,128)S(1)}, f32[2,136,1152]{2,1,0:T(8,128)}, u32[]{:S(2)}) copy-start(f32[2,136,1152]{2,1,0:T(8,128)} %get-tuple-element.702) | copy-start | bytes 3760132 | tf_op jit(solution)/shard_map/while
  61.6 2.5 %copy-start.3 = (f32[2,136,1152]{2,1,0:T(8,128)S(1)}, f32[2,136,1152]{2,1,0:T(8,128)}, u32[]{:S(2)}) copy-start(f32[2,136,1152]{2,1,0:T(8,128)} %get-tuple-element.703) | copy-start | bytes 3760132 | tf_op jit(solution)/shard_map/while
  75.4 1.9 copy-start.7
  75.5 2.2 %copy-start.1 = (f32[2,136,1152]{2,1,0:T(8,128)S(1)}, f32[2,136,1152]{2,1,0:T(8,128)}, u32[]{:S(2)}) copy-start(f32[2,136,1152]{2,1,0:T(8,128)} %get-tuple-element.702) | copy-start | bytes 3760132 | tf_op jit(solution)/shard_map/while
  75.5 2.5 %copy-start.3 = (f32[2,136,1152]{2,1,0:T(8,128)S(1)}, f32[2,136,1152]{2,1,0:T(8,128)}, u32[]{:S(2)}) copy-start(f32[2,136,1152]{2,1,0:T(8,128)} %get-tuple-element.703) | copy-start | bytes 3760132 | tf_op jit(solution)/shard_map/while
  89.3 1.9 copy-start.7
  89.4 2.2 %copy-start.1 = (f32[2,136,1152]{2,1,0:T(8,128)S(1)}, f32[2,136,1152]{2,1,0:T(8,128)}, u32[]{:S(2)}) copy-start(f32[2,136,1152]{2,1,0:T(8,128)} %get-tuple-element.702) | copy-start | bytes 3760132 | tf_op jit(solution)/shard_map/while
  89.4 2.5 %copy-start.3 = (f32[2,136,1152]{2,1,0:T(8,128)S(1)}, f32[2,136,1152]{2,1,0:T(8,128)}, u32[]{:S(2)}) copy-start(f32[2,136,1152]{2,1,0:T(8,128)} %get-tuple-element.703) | copy-start | bytes 3760132 | tf_op jit(solution)/shard_map/while
  103.2 1.9 copy-start.7
  103.3 2.2 %copy-start.1 = (f32[2,136,1152]{2,1,0:T(8,128)S(1)}, f32[2,136,1152]{2,1,0:T(8,128)}, u32[]{:S(2)}) copy-start(f32[2,136,1152]{2,1,0:T(8,128)} %get-tuple-element.702) | copy-start | bytes 3760132 | tf_op jit(solution)/shard_map/while
  103.3 2.5 %copy-start.3 = (f32[2,136,1152]{2,1,0:T(8,128)S(1)}, f32[2,136,1152]{2,1,0:T(8,128)}, u32[]{:S(2)}) copy-start(f32[2,136,1152]{2,1,0:T(8,128)} %get-tuple-element.703) | copy-start | bytes 3760132 | tf_op jit(solution)/shard_map/while
  117.1 1.9 copy-start.7
  117.2 2.2 %copy-start.1 = (f32[2,136,1152]{2,1,0:T(8,128)S(1)}, f32[2,136,1152]{2,1,0:T(8,128)}, u32[]{:S(2)}) copy-start(f32[2,136,1152]{2,1,0:T(8,128)} %get-tuple-element.702) | copy-start | bytes 3760132 | tf_op jit(solution)/shard_map/while
  117.2 2.5 %copy-start.3 = (f32[2,136,1152]{2,1,0:T(8,128)S(1)}, f32[2,136,1152]{2,1,0:T(8,128)}, u32[]{:S(2)}) copy-start(f32[2,136,1152]{2,1,0:T(8,128)} %get-tuple-element.703) | copy-start | bytes 3760132 | tf_op jit(solution)/shard_map/while
  131.1 2.2 %copy-start.1 = (f32[2,136,1152]{2,1,0:T(8,128)S(1)}, f32[2,136,1152]{2,1,0:T(8,128)}, u32[]{:S(2)}) copy-start(f32[2,136,1152]{2,1,0:T(8,128)} %get-tuple-element.702) | copy-start | bytes 3760132 | tf_op jit(solution)/shard_map/while
  131.1 2.5 %copy-start.3 = (f32[2,136,1152]{2,1,0:T(8,128)S(1)}, f32[2,136,1152]{2,1,0:T(8,128)}, u32[]{:S(2)}) copy-start(f32[2,136,1152]{2,1,0:T(8,128)} %get-tuple-element.703) | copy-start | bytes 3760132 | tf_op jit(solution)/shard_map/while
  145.0 2.2 %copy-start.1 = (f32[2,136,1152]{2,1,0:T(8,128)S(1)}, f32[2,136,1152]{2,1,0:T(8,128)}, u32[]{:S(2)}) copy-start(f32[2,136,1152]{2,1,0:T(8,128)} %get-tuple-element.702) | copy-start | bytes 3760132 | tf_op jit(solution)/shard_map/while
  145.0 2.5 %copy-start.3 = (f32[2,136,1152]{2,1,0:T(8,128)S(1)}, f32[2,136,1152]{2,1,0:T(8,128)}, u32[]{:S(2)}) copy-start(f32[2,136,1152]{2,1,0:T(8,128)} %get-tuple-element.703) | copy-start | bytes 3760132 | tf_op jit(solution)/shard_map/while
  (22 other events, 31.4 us)
